TPU v7x, 32 devices: a whole 2x2x4 slice. The times are simulated.
32 devices in a mesh: lat: 8 (over z, core), lon: 4 (over y, x).
Axes of the slice: x: 2, y: 2, z: 4, core: 2. Of those that a mesh axis runs over, the one named last changes fastest.
Arguments:
- predicted_state: float32 [1440, 13312], P('lon', 'lat'), may hold values from -24 to 24
- verified_state: float32 [1440, 13312], P('lon', 'lat'), may hold values from -20 to 20
- normal_state: float32 [1440, 13312], P('lon', 'lat'), may hold values from -3 to 3
Outputs:
- energy_curves: float32 [3, 52, 721], replicated
- rms_error: float32 [52], replicated
- anomaly_corr: float32 [52], replicated
All inputs are finite; a program needn't handle non-finite values.
Results may differ from a plain program's by a relative error of at most 0.00005.
Values sent between devices are 32-bit elements; how exact they have to be, the bound alone decides.
A program may use at most 64 MiB of HBM per device.

v0:
```python
import jax
import jax.numpy as jnp
from jax import lax
from jax.sharding import PartitionSpec as P

FIELDS = 52
epsilon = 1e-06


def latitude_weights(lat_index, parallel_number):
    return jnp.cos(jnp.pi * ((lat_index.astype(jnp.float32) + 0.5) / parallel_number - 0.5))


def dft_table(lon_rows, lon_total, wave_count):
    longitudes = jnp.arange(lon_rows, dtype=jnp.int32)
    waves = jnp.arange(wave_count, dtype=jnp.int32)
    phase = longitudes[:, None] * waves[None, :] % lon_total
    angle = 2.0 * jnp.pi / lon_total * phase.astype(jnp.float32)
    return jnp.concatenate([jnp.cos(angle), -jnp.sin(angle)], axis=1)


def transform_columns(stacked, table):
    return lax.dot_general(
        stacked,
        table,
        (((0,), (0,)), ((), ())),
        precision=lax.Precision.HIGHEST,
        preferred_element_type=jnp.float32,
    )


def row_powers(fore_coeffs, true_coeffs, wave_count):
    diff_coeffs = fore_coeffs - true_coeffs

    def square(coeffs):
        return (
            coeffs[:, :wave_count] * coeffs[:, :wave_count]
            + coeffs[:, wave_count:] * coeffs[:, wave_count:]
        )

    return jnp.stack([square(fore_coeffs), square(true_coeffs), square(diff_coeffs)], axis=1)


def local(predicted_state, verified_state, normal_state):
    quantity_labels = FIELDS
    meridian_lines, meridian_number = predicted_state.shape
    parallel_lines = meridian_number // quantity_labels
    parallel_number = parallel_lines * lax.axis_size("lat")
    lon_devices = lax.axis_size("lon")
    lon_total = meridian_lines * lon_devices
    wave_count = lon_total // 2 + 1
    row_share = meridian_number // lon_devices
    lat_first = lax.axis_index("lat") * parallel_lines
    weights = latitude_weights(
        lat_first + jnp.arange(parallel_lines, dtype=jnp.int32), parallel_number
    )
    weight_total = jnp.sum(
        latitude_weights(jnp.arange(parallel_number, dtype=jnp.int32), parallel_number)
    )
    predicted_block = predicted_state.reshape(meridian_lines, parallel_lines, quantity_labels)
    observed_block = verified_state.reshape(meridian_lines, parallel_lines, quantity_labels)
    normal_block = normal_state.reshape(meridian_lines, parallel_lines, quantity_labels)
    mismatch_parts = predicted_block - observed_block
    predicted_anomalies = predicted_block - normal_block
    observed_anomalies = observed_block - normal_block
    broad_layout = weights[None, :, None]
    skill_terms = jnp.stack(
        [
            jnp.sum(broad_layout * mismatch_parts * mismatch_parts, axis=(0, 1)),
            jnp.sum(broad_layout * predicted_anomalies * observed_anomalies, axis=(0, 1)),
            jnp.sum(broad_layout * predicted_anomalies * predicted_anomalies, axis=(0, 1)),
            jnp.sum(broad_layout * observed_anomalies * observed_anomalies, axis=(0, 1)),
        ]
    )
    predicted_meridians = predicted_block.transpose(0, 2, 1).reshape(
        meridian_lines, meridian_number
    )
    true_cols = observed_block.transpose(0, 2, 1).reshape(meridian_lines, meridian_number)
    full_table = dft_table(lon_total, lon_total, wave_count)
    fore_blocks = predicted_meridians.reshape(meridian_lines, lon_devices, row_share)
    true_blocks = true_cols.reshape(meridian_lines, lon_devices, row_share)
    fore_part = lax.all_to_all(fore_blocks, "lon", split_axis=1, concat_axis=0, tiled=True)[:, 0, :]
    true_part = lax.all_to_all(true_blocks, "lon", split_axis=1, concat_axis=0, tiled=True)[:, 0, :]
    items = fore_part.shape[1]
    stacked = jnp.concatenate([fore_part, true_part], axis=1)
    coeffs = transform_columns(stacked, full_table)
    powers = row_powers(coeffs[:items], coeffs[items:], wave_count)
    share_start = lax.axis_index("lon") * row_share
    global_cols = share_start + jnp.arange(row_share, dtype=jnp.int32)
    field_of = global_cols // parallel_lines
    row_weights = latitude_weights(lat_first + global_cols % parallel_lines, parallel_number)
    row_scale = row_weights / (lon_total * lon_total * weight_total)
    weighted = powers.reshape(row_share, 3 * wave_count) * row_scale[:, None]
    field_index = jnp.arange(quantity_labels, dtype=jnp.int32)
    window = min(quantity_labels, row_share // parallel_lines + 2)
    first_field = share_start // parallel_lines
    window_index = jnp.arange(window, dtype=jnp.int32)
    offset = field_of - first_field
    selector = (offset[None, :] == window_index[:, None]).astype(jnp.float32)
    band_sum = jnp.dot(
        selector, weighted, precision=lax.Precision.HIGHEST, preferred_element_type=jnp.float32
    )
    band_sum = lax.psum(band_sum, "lat")
    gathered = lax.all_gather(band_sum, "lon", axis=0, tiled=True)
    slot_index = jnp.arange(lon_devices * window, dtype=jnp.int32)
    slot_field = slot_index // window * row_share // parallel_lines + slot_index % window
    placer = (slot_field[None, :] == field_index[:, None]).astype(jnp.float32)
    summed = jnp.dot(
        placer, gathered, precision=lax.Precision.HIGHEST, preferred_element_type=jnp.float32
    )
    energy_curves = summed.reshape(quantity_labels, 3, wave_count).transpose(1, 0, 2)
    skill_means = lax.psum(skill_terms, ("lat", "lon")) / (lon_total * weight_total)
    rms_error = jnp.sqrt(skill_means[0])
    anomaly_corr = skill_means[1] / jnp.sqrt(
        (skill_means[2] + epsilon) * (skill_means[3] + epsilon)
    )
    return (energy_curves, rms_error, anomaly_corr)


def solution(mesh):
    in_specs = (P("lon", "lat"), P("lon", "lat"), P("lon", "lat"))
    out_specs = (P(), P(), P())
    return jax.shard_map(local, mesh=mesh, in_specs=in_specs, out_specs=out_specs, check_vma=False)
```

profile of v0, /device:TPU:8, one launch (start us, length us, event | category | flops | bytes accessed | tf_op | source)
XLA Modules:
  0.0 275.4 jit_solution(18060614692774121550)
XLA Ops:
  7.2 3.2 %copy.26 = f32[360,1664]{0,1:T(8,128)} copy(f32[360,1664]{1,0:T(8,128)} %param.4) | data formatting | bytes 4792320 | tf_op args[1]
  10.4 2.4 reshape.125
  12.8 1.9 copy.27
  14.8 4.8 %all-to-all-start.1 = ((f32[360,4,416]{0,2,1:T(8,128)}), f32[360,4,416]{0,2,1:T(8,128)}, u32[]{:S(2)}, u32[]{:S(2)}) async-start(f32[360,4,416]{0,2,1:T(8,128)} %bitcast.41), calls=%async_computation.1 | async-start | bytes 5111808 | tf_op jit(solution)/shard_map/all_to_all | solution.py:83
  19.6 2.2 copy.23
  21.7 2.4 reshape.124
  24.2 2.1 copy.24
  26.5 23.2 %all-to-all-done.1 = f32[360,4,416]{0,2,1:T(8,128)} async-done(((f32[360,4,416]{0,2,1:T(8,128)}), f32[360,4,416]{0,2,1:T(8,128)}, u32[]{:S(2)}, u32[]{:S(2)}) %all-to-all-start.1) | async-done | bytes 2396192 | tf_op jit(solution)/shard_map/all_to_all | solution.py:83
  49.7 3.6 %all-to-all-start = ((f32[360,4,416]{0,2,1:T(8,128)}), f32[360,4,416]{0,2,1:T(8,128)S(1)}, u32[]{:S(2)}, u32[]{:S(2)}) async-start(f32[360,4,416]{0,2,1:T(8,128)} %bitcast.39), calls=%async_computation | async-start | bytes 5111808 | tf_op jit(solution)/shard_map/all_to_all | solution.py:82
  53.4 4.3 %fusion.17 = (f32[1664]{0:T(1024)S(1)}, f32[1664]{0:T(1024)S(1)}, f32[1664]{0:T(1024)S(1)}, f32[1664]{0:T(1024)S(1)}) fusion(f32[360,1664]{1,0:T(8,128)} %param.3, f32[360,1664]{1,0:T(8,128)} %param.4, f32[1664]{0:T(1024)S(1)} %mul.171, f32[360,1664]{1,0:T(8,128)} %param.5), kind=kLoop, calls=%fused_computation.26 | loop fusion | flops 8379904 | bytes 7221760 | tf_op jit(solution)/shard_map/reduce_sum | solution.py:69
  60.1 55.8 %psum.15 = f32[4,52]{1,0:T(4,128)S(1)} all-reduce(f32[4,52]{1,0:T(4,128)S(1)} %pad_maximum_fusion.1), channel_id=1, replica_groups=mesh['lat'=8,'lon'=4] {'lat','lon'}, use_global_device_ids=true, to_apply=%region_10.11 | all-reduce | flops 208 | bytes 1664 | tf_op jit(solution)/shard_map/psum | solution.py:112
  116.5 19.7 %sine_negate_fusion = (f32[1440,721]{1,0:T(8,128)}, f32[1440,721]{1,0:T(8,128)}) fusion(), kind=kLoop, calls=%fused_computation.12 | loop fusion | flops 10382400 | bytes 8305920 | tf_op jit(solution)/shard_map/neg | solution.py:19
  136.2 4.8 %copy.28 = f32[4,360,1,416]{1,0,3,2:T(4,128)} copy(f32[4,360,1,416]{1,3,0,2:T(8,128)} %bitcast.7) | data formatting | bytes 4792320 | tf_op jit(solution)/shard_map/all_to_all | solution.py:83
  141.1 4.0 %squeeze.5 = f32[1440,416]{0,1:T(8,128)} reshape(f32[4,360,1,416]{1,0,3,2:T(4,128)} %copy.28) | data formatting | bytes 4792320 | tf_op jit(solution)/shard_map/squeeze | solution.py:83
  145.1 3.1 %copy.25 = f32[4,360,1,416]{1,0,3,2:T(4,128)} copy(f32[4,360,1,416]{1,3,0,2:T(8,128)S(1)} %bitcast.40) | data formatting | bytes 4792320 | tf_op jit(solution)/shard_map/all_to_all | solution.py:82
  148.2 4.2 %squeeze.4 = f32[1440,416]{0,1:T(8,128)} reshape(f32[4,360,1,416]{1,0,3,2:T(4,128)} %copy.25) | data formatting | bytes 4792320 | tf_op jit(solution)/shard_map/squeeze | solution.py:82
  152.4 29.4 %fusion = f32[832,1442]{1,0:T(8,128)S(1)} fusion(f32[1440,721]{1,0:T(8,128)} %get-tuple-element.20, f32[1440,721]{1,0:T(8,128)} %get-tuple-element.21, f32[1440,416]{0,1:T(8,128)S(1)} %copy-done.1, f32[1440,416]{0,1:T(8,128)} %squeeze.4), kind=kOutput, calls=%fused_computation | convolution fusion | flops 20734851072 | bytes 17897216 | tf_op jit(solution)/shard_map/dot_general | solution.py:23
  183.4 2.1 pad_maximum_fusion
  185.5 5.6 %copy.29 = f32[416,3,721]{0,2,1:T(8,128)} copy(f32[416,3,721]{2,0,1:T(8,128)} %pad_maximum_fusion) | data formatting | bytes 7198464 | tf_op jit(solution)/shard_map/stack | solution.py:41
  191.1 4.9 %reshape.126 = f32[416,2163]{0,1:T(8,128)} reshape(f32[416,3,721]{0,2,1:T(8,128)} %copy.29) | data formatting | bytes 7198464 | tf_op jit(solution)/shard_map/reshape | solution.py:93
  196.0 5.2 %fusion.7 = f32[15,2163]{1,0:T(8,128)} fusion(f32[416,2163]{0,1:T(8,128)} %reshape.126, f32[416]{0:T(512)S(1)} %fusion.37, s32[416]{0:T(512)S(1)} %fusion.29), kind=kOutput, calls=%fused_computation.8 | convolution fusion | flops 162871488 | bytes 3732340 | tf_op jit(solution)/shard_map/dot_general | solution.py:100
  201.2 54.4 %all-reduce.2.cloned.1.call-done = f32[15,2163]{1,0:T(8,128)} async-done(((f32[15,2163]{1,0:T(8,128)}), f32[15,2163]{1,0:T(8,128)}) %all-reduce.2.cloned.1.call-update) | async-done | bytes 129796 | tf_op jit(solution)/shard_map/psum | solution.py:103
  255.6 11.1 %all-gather = f32[4,15,2163]{2,1,0:T(8,128)S(1)} all-gather(f32[1,15,2163]{2,1,0:T(8,128)} %bitcast.43), channel_id=1, replica_groups=mesh['lat'=8,'lon'=4] {'lon'}, dimensions={0}, use_global_device_ids=true | all-gather | bytes 648900 | tf_op jit(solution)/shard_map/all_gather | solution.py:104
  267.7 0.9 copy.30
  (31 shorter events, 4.5 us)
Async XLA Ops:
  14.8 4.8 %copy-start = (f32[360,1664]{1,0:T(8,128)S(1)}, f32[360,1664]{1,0:T(8,128)}, u32[]{:S(2)}) copy-start(f32[360,1664]{1,0:T(8,128)} %param.3) | copy-start | bytes 7188484
  14.8 34.9 %all-to-all-start.1 = ((f32[360,4,416]{0,2,1:T(8,128)}), f32[360,4,416]{0,2,1:T(8,128)}, u32[]{:S(2)}, u32[]{:S(2)}) async-start(f32[360,4,416]{0,2,1:T(8,128)} %bitcast.41), calls=%async_computation.1 | async-start | bytes 5111808 | tf_op jit(solution)/shard_map/all_to_all | solution.py:83
  49.7 95.4 %all-to-all-start = ((f32[360,4,416]{0,2,1:T(8,128)}), f32[360,4,416]{0,2,1:T(8,128)S(1)}, u32[]{:S(2)}, u32[]{:S(2)}) async-start(f32[360,4,416]{0,2,1:T(8,128)} %bitcast.39), calls=%async_computation | async-start | bytes 5111808 | tf_op jit(solution)/shard_map/all_to_all | solution.py:82
  53.3 202.3 %all-reduce.2.cloned.1.call-start = ((), (), s32[]{:S(2)}) async-start(), calls=%async_computation.2 | async-start | bytes 278528 | tf_op jit(solution)/shard_map/psum | solution.py:103
  148.2 4.2 %copy-start.1 = (f32[1440,416]{0,1:T(8,128)S(1)}, f32[1440,416]{0,1:T(8,128)}, u32[]{:S(2)}) copy-start(f32[1440,416]{0,1:T(8,128)} %squeeze.5) | copy-start | bytes 7188484
Sparse Core Ops, SparseCore 0:
  201.3 54.3 all-reduce.1
where the time goes:
time: 276 us; the launch traced here: 275 us
  waiting for transfers between devices  77.7 us (28%)
  blocking collectives  66.9 us (24%)
  local copies, waits for them, and re-layouts  42.9 us (16%)
  matrix products  35 us (13%)
  other arithmetic  29 us (11%)
  between operations  15.5 us (6%)
  starting transfers between devices  8.44 us (3%)
    psum x1, blocking collectives, local(): lax.psum(skill_terms, ('lat', 'lon')) / (lon_total * weight_total)  55.8 us
    psum x1, waiting for transfers between devices, local(): band_sum = lax.psum(band_sum, 'lat')  54.4 us
    dot_general x1, matrix products, transform_columns(): lax.dot_general(stacked, table, (((0,), (0,)), ((), ())), precision=lax.P...  29.4 us
    all_to_all x1, waiting for transfers between devices, local(): lax.all_to_all(true_blocks, 'lon', split_axis=1, concat_axis=0, tiled=True)  23.2 us
    neg x1, other arithmetic, dft_table(): return jnp.concatenate([jnp.cos(angle), -jnp.sin(angle)], axis=1)  19.7 us
    all_gather x1, blocking collectives, local(): gathered = lax.all_gather(band_sum, 'lon', axis=0, tiled=True)  11.1 us
    unnamed x8, local copies, waits for them, and re-layouts  6.34 us
    another operation x1, local copies, waits for them, and re-layouts, row_powers(): jnp.stack([square(fore_coeffs), square(true_coeffs), square(diff_coeffs)]...  5.61 us
  transfers between devices with their start and end apart: 3, of which 2 were waited for; matrix products, arithmetic and copies ran while one was open for 15% of the time, Pallas kernels for 0%

commit v1 on v0

--- a/solution.py
+++ b/solution.py
@@ -100,7 +100,9 @@
     band_sum = jnp.dot(
         selector, weighted, precision=lax.Precision.HIGHEST, preferred_element_type=jnp.float32
     )
-    band_sum = lax.psum(band_sum, "lat")
+    band_sum = band_sum
+    for hop in (1, 2, 4):
+        band_sum = band_sum + lax.ppermute(band_sum, "lat", [(dev, dev ^ hop) for dev in range(8)])
     gathered = lax.all_gather(band_sum, "lon", axis=0, tiled=True)
     slot_index = jnp.arange(lon_devices * window, dtype=jnp.int32)
     slot_field = slot_index // window * row_share // parallel_lines + slot_index % window

time: 276 us -> 205 us (0.74)
  waiting for transfers between devices: 77.7 us -> 32.2 us
  blocking collectives: 66.9 us -> 51.8 us
  between operations: 15.5 us -> 2.14 us
    psum x1 -> x0, waiting for transfers between devices: 54.4 us -> none  [local(): band_sum = lax.psum(band_sum, 'lat')]
    psum x1, blocking collectives: 55.8 us -> 40.9 us  [local(): lax.psum(skill_terms, ('lat', 'lon')) / (lon_total * weight_total)]
    ppermute x0 -> x3, waiting for transfers between devices: none -> 8.8 us  [local(): lax.ppermute(band_sum, 'lat', [(dev, dev ^ hop) for dev in range(8)])]
    unnamed x8 -> x12, local copies, waits for them, and re-layouts: 6.34 us -> 6.35 us
  transfers between devices with their start and end apart: 3 -> 5, of which waited for: 2 -> 3; matrix products, arithmetic and copies ran while one was open for 15% -> 20% of each run, Pallas kernels for 0% -> 0%
where the time goes in v1:
time: 205 us; the launch traced here: 202 us
  blocking collectives  51.8 us (25%)
  local copies, waits for them, and re-layouts  43 us (21%)
  matrix products  34.5 us (17%)
  waiting for transfers between devices  32.2 us (16%)
  other arithmetic  27.6 us (13%)
  starting transfers between devices  10.3 us (5%)
  between operations  2.14 us (1%)
    psum x1, blocking collectives, local(): lax.psum(skill_terms, ('lat', 'lon')) / (lon_total * weight_total)  40.9 us
    dot_general x1, matrix products, transform_columns(): lax.dot_general(stacked, table, (((0,), (0,)), ((), ())), precision=lax.P...  29.4 us
    all_to_all x1, waiting for transfers between devices, local(): lax.all_to_all(true_blocks, 'lon', split_axis=1, concat_axis=0, tiled=True)  23.4 us
    neg x1, other arithmetic, dft_table(): return jnp.concatenate([jnp.cos(angle), -jnp.sin(angle)], axis=1)  19.7 us
    all_gather x1, blocking collectives, local(): gathered = lax.all_gather(band_sum, 'lon', axis=0, tiled=True)  10.9 us
    ppermute x3, waiting for transfers between devices, local(): lax.ppermute(band_sum, 'lat', [(dev, dev ^ hop) for dev in range(8)])  8.8 us
    unnamed x12, local copies, waits for them, and re-layouts  6.35 us
    another operation x1, local copies, waits for them, and re-layouts, row_powers(): jnp.stack([square(fore_coeffs), square(true_coeffs), square(diff_coeffs)]...  5.61 us
  transfers between devices with their start and end apart: 5, of which 3 were waited for; matrix products, arithmetic and copies ran while one was open for 20% of the time, Pallas kernels for 0%

profile of v1, /device:TPU:8, one launch (start us, length us, event | category | flops | bytes accessed | tf_op | source)
XLA Modules:
  0.0 201.7 jit_solution(15554190356681933000)
XLA Ops:
  0.6 3.2 %copy.26 = f32[360,1664]{0,1:T(8,128)} copy(f32[360,1664]{1,0:T(8,128)} %param.4) | data formatting | bytes 4792320 | tf_op args[1]
  3.9 2.4 %reshape.125 = f32[360,32,52]{0,2,1:T(8,128)S(1)} reshape(f32[360,1664]{0,1:T(8,128)} %copy.26) | data formatting | bytes 4792320 | tf_op jit(solution)/shard_map/reshape | solution.py:61
  6.3 1.9 copy.27
  8.2 4.8 %all-to-all-start.1 = ((f32[360,4,416]{0,2,1:T(8,128)}), f32[360,4,416]{0,2,1:T(8,128)}, u32[]{:S(2)}, u32[]{:S(2)}) async-start(f32[360,4,416]{0,2,1:T(8,128)} %bitcast.42), calls=%async_computation.1 | async-start | bytes 5111808 | tf_op jit(solution)/shard_map/all_to_all | solution.py:83
  13.0 2.2 %copy.23 = f32[360,1664]{0,1:T(8,128)} copy(f32[360,1664]{1,0:T(8,128)S(1)} %copy-done.1) | data formatting | bytes 4792320 | tf_op args[0]
  15.2 2.4 %reshape.124 = f32[360,32,52]{0,2,1:T(8,128)S(1)} reshape(f32[360,1664]{0,1:T(8,128)} %copy.23) | data formatting | bytes 4792320 | tf_op jit(solution)/shard_map/reshape | solution.py:60
  17.6 2.1 %copy.24 = f32[360,52,32]{0,2,1:T(8,128)} copy(f32[360,52,32]{0,1,2:T(8,128)S(1)} %bitcast.39) | data formatting | bytes 4792320 | tf_op jit(solution)/shard_map/transpose | solution.py:75
  19.7 23.4 %all-to-all-done.1 = f32[360,4,416]{0,2,1:T(8,128)} async-done(((f32[360,4,416]{0,2,1:T(8,128)}), f32[360,4,416]{0,2,1:T(8,128)}, u32[]{:S(2)}, u32[]{:S(2)}) %all-to-all-start.1) | async-done | bytes 2396192 | tf_op jit(solution)/shard_map/all_to_all | solution.py:83
  43.1 3.6 %all-to-all-start = ((f32[360,4,416]{0,2,1:T(8,128)}), f32[360,4,416]{0,2,1:T(8,128)S(1)}, u32[]{:S(2)}, u32[]{:S(2)}) async-start(f32[360,4,416]{0,2,1:T(8,128)} %bitcast.40), calls=%async_computation | async-start | bytes 5111808 | tf_op jit(solution)/shard_map/all_to_all | solution.py:82
  48.4 19.7 %sine_negate_fusion = (f32[1440,721]{1,0:T(8,128)}, f32[1440,721]{1,0:T(8,128)}) fusion(), kind=kLoop, calls=%fused_computation.12 | loop fusion | flops 10382400 | bytes 8305920 | tf_op jit(solution)/shard_map/neg | solution.py:19
  68.1 4.8 %copy.28 = f32[4,360,1,416]{1,0,3,2:T(4,128)} copy(f32[4,360,1,416]{1,3,0,2:T(8,128)} %bitcast.7) | data formatting | bytes 4792320 | tf_op jit(solution)/shard_map/all_to_all | solution.py:83
  72.9 4.0 %squeeze.5 = f32[1440,416]{0,1:T(8,128)} reshape(f32[4,360,1,416]{1,0,3,2:T(4,128)} %copy.28) | data formatting | bytes 4792320 | tf_op jit(solution)/shard_map/squeeze | solution.py:83
  77.0 3.1 %copy.25 = f32[4,360,1,416]{1,0,3,2:T(4,128)} copy(f32[4,360,1,416]{1,3,0,2:T(8,128)S(1)} %bitcast.41) | data formatting | bytes 4792320 | tf_op jit(solution)/shard_map/all_to_all | solution.py:82
  80.1 4.2 %squeeze.4 = f32[1440,416]{0,1:T(8,128)} reshape(f32[4,360,1,416]{1,0,3,2:T(4,128)} %copy.25) | data formatting | bytes 4792320 | tf_op jit(solution)/shard_map/squeeze | solution.py:82
  84.3 29.4 %fusion = f32[832,1442]{1,0:T(8,128)S(1)} fusion(f32[1440,721]{1,0:T(8,128)} %get-tuple-element.20, f32[1440,721]{1,0:T(8,128)} %get-tuple-element.21, f32[1440,416]{0,1:T(8,128)S(1)} %copy-done.3, f32[1440,416]{0,1:T(8,128)} %squeeze.4), kind=kOutput, calls=%fused_computation | convolution fusion | flops 20734851072 | bytes 17897216 | tf_op jit(solution)/shard_map/dot_general | solution.py:23
  115.3 2.1 %pad_maximum_fusion = f32[416,3,721]{2,0,1:T(8,128)} fusion(f32[416,1,721]{2,0,1:T(8,128)S(1)} %fusion.21, f32[416,1,721]{2,0,1:T(8,128)S(1)} %get-tuple-element.17, f32[416,1,721]{2,0,1:T(8,128)S(1)} %get-tuple-element.16), kind=kLoop, calls=%fused_computation.18 | loop fusion | flops 1799616 | bytes 7198464 | tf_op jit(solution)/shard_map/stack | solution.py:41
  117.4 5.6 %copy.29 = f32[416,3,721]{0,2,1:T(8,128)} copy(f32[416,3,721]{2,0,1:T(8,128)} %pad_maximum_fusion) | data formatting | bytes 7198464 | tf_op jit(solution)/shard_map/stack | solution.py:41
  123.0 5.0 %reshape.126 = f32[416,2163]{0,1:T(8,128)} reshape(f32[416,3,721]{0,2,1:T(8,128)} %copy.29) | data formatting | bytes 7198464 | tf_op jit(solution)/shard_map/reshape | solution.py:93
  128.0 4.6 %fusion.7 = f32[15,2163]{1,0:T(8,128)S(1)} fusion(f32[416,2163]{0,1:T(8,128)} %reshape.126, f32[416]{0:T(512)S(1)} %fusion.37, s32[416]{0:T(512)S(1)} %fusion.29), kind=kOutput, calls=%fused_computation.8 | convolution fusion | flops 162871488 | bytes 3732340 | tf_op jit(solution)/shard_map/dot_general | solution.py:100
  132.7 2.8 %fusion.17 = (f32[1664]{0:T(1024)S(1)}, f32[1664]{0:T(1024)S(1)}, f32[1664]{0:T(1024)S(1)}, f32[1664]{0:T(1024)S(1)}) fusion(f32[360,1664]{1,0:T(8,128)S(1)} %copy-done.2, f32[360,1664]{1,0:T(8,128)S(1)} %copy-done, f32[1664]{0:T(1024)S(1)} %mul.171, f32[360,1664]{1,0:T(8,128)} %param.5), kind=kLoop, calls=%fused_computation.26 | loop fusion | flops 8379904 | bytes 7221760 | tf_op jit(solution)/shard_map/reduce_sum | solution.py:69
  136.7 40.9 %psum.7 = f32[4,52]{1,0:T(4,128)S(1)} all-reduce(f32[4,52]{1,0:T(4,128)S(1)} %pad_maximum_fusion.1), channel_id=1, replica_groups=mesh['lat'=8,'lon'=4] {'lat','lon'}, use_global_device_ids=true, to_apply=%region_9.10 | all-reduce | flops 208 | bytes 1664 | tf_op jit(solution)/shard_map/psum | solution.py:114
  178.2 4.5 %collective-permute-done.1 = f32[15,2163]{1,0:T(8,128)S(1)} collective-permute-done((f32[15,2163]{1,0:T(8,128)S(1)}, f32[15,2163]{1,0:T(8,128)S(1)}, u32[]{:S(2)}, u32[]{:S(2)}) %collective-permute-start.1) | collective-permute-done | bytes 129812 | tf_op jit(solution)/shard_map/ppermute | solution.py:105
  184.6 4.3 %collective-permute-done.2 = f32[15,2163]{1,0:T(8,128)S(1)} collective-permute-done((f32[15,2163]{1,0:T(8,128)S(1)}, f32[15,2163]{1,0:T(8,128)S(1)}, u32[]{:S(2)}, u32[]{:S(2)}) %collective-permute-start.2) | collective-permute-done | bytes 129812 | tf_op jit(solution)/shard_map/ppermute | solution.py:105
  188.9 10.9 %all-gather = f32[4,15,2163]{2,1,0:T(8,128)S(1)} all-gather(f32[1,15,2163]{2,1,0:T(8,128)S(1)} %add_bitcast_fusion), channel_id=1, replica_groups=mesh['lat'=8,'lon'=4] {'lon'}, dimensions={0}, use_global_device_ids=true | all-gather | bytes 648900 | tf_op jit(solution)/shard_map/all_gather | solution.py:106
  (41 shorter events, 7.3 us)
Async XLA Ops:
  8.2 4.8 %copy-start.1 = (f32[360,1664]{1,0:T(8,128)S(1)}, f32[360,1664]{1,0:T(8,128)}, u32[]{:S(2)}) copy-start(f32[360,1664]{1,0:T(8,128)} %param.3) | copy-start | bytes 7188484
  8.2 34.9 %all-to-all-start.1 = ((f32[360,4,416]{0,2,1:T(8,128)}), f32[360,4,416]{0,2,1:T(8,128)}, u32[]{:S(2)}, u32[]{:S(2)}) async-start(f32[360,4,416]{0,2,1:T(8,128)} %bitcast.42), calls=%async_computation.1 | async-start | bytes 5111808 | tf_op jit(solution)/shard_map/all_to_all | solution.py:83
  43.1 33.9 %all-to-all-start = ((f32[360,4,416]{0,2,1:T(8,128)}), f32[360,4,416]{0,2,1:T(8,128)S(1)}, u32[]{:S(2)}, u32[]{:S(2)}) async-start(f32[360,4,416]{0,2,1:T(8,128)} %bitcast.40), calls=%async_computation | async-start | bytes 5111808 | tf_op jit(solution)/shard_map/all_to_all | solution.py:82
  80.1 4.2 %copy-start.3 = (f32[1440,416]{0,1:T(8,128)S(1)}, f32[1440,416]{0,1:T(8,128)}, u32[]{:S(2)}) copy-start(f32[1440,416]{0,1:T(8,128)} %squeeze.5) | copy-start | bytes 7188484
  123.0 9.7 %copy-start.2 = (f32[360,1664]{1,0:T(8,128)S(1)}, f32[360,1664]{1,0:T(8,128)}, u32[]{:S(2)}) copy-start(f32[360,1664]{1,0:T(8,128)} %param.3) | copy-start | bytes 7188484
  128.0 4.7 %copy-start = (f32[360,1664]{1,0:T(8,128)S(1)}, f32[360,1664]{1,0:T(8,128)}, u32[]{:S(2)}) copy-start(f32[360,1664]{1,0:T(8,128)} %param.4) | copy-start | bytes 7188484
  132.7 44.9 %collective-permute-start = (f32[15,2163]{1,0:T(8,128)S(1)}, f32[15,2163]{1,0:T(8,128)S(1)}, u32[]{:S(2)}, u32[]{:S(2)}) collective-permute-start(f32[15,2163]{1,0:T(8,128)S(1)} %fusion.7), channel_id=1, source_target_pairs={{0,4},{4,0},{8,12},{12,8},{16,20},{20,16},{24,28},{28,24},{1,5},{5... | collective-permute-start | bytes 389348 | tf_op jit(solution)/shard_map/ppermute | solution.py:105
  177.6 5.1 %collective-permute-start.1 = (f32[15,2163]{1,0:T(8,128)S(1)}, f32[15,2163]{1,0:T(8,128)S(1)}, u32[]{:S(2)}, u32[]{:S(2)}) collective-permute-start(f32[15,2163]{1,0:T(8,128)S(1)} %add.154), channel_id=1, source_target_pairs={{0,8},{4,12},{8,0},{12,4},{16,24},{20,28},{24,16},{28,20},{1,9},{5... | collective-permute-start | bytes 389348 | tf_op jit(solution)/shard_map/ppermute | solution.py:105
  182.8 6.1 %collective-permute-start.2 = (f32[15,2163]{1,0:T(8,128)S(1)}, f32[15,2163]{1,0:T(8,128)S(1)}, u32[]{:S(2)}, u32[]{:S(2)}) collective-permute-start(f32[15,2163]{1,0:T(8,128)S(1)} %add.155), channel_id=1, source_target_pairs={{0,16},{4,20},{8,24},{12,28},{16,0},{20,4},{24,8},{28,12},{1,17},{... | collective-permute-start | bytes 389348 | tf_op jit(solution)/shard_map/ppermute | solution.py:105
